TPU v7x, 32 devices: a whole 2x2x4 slice. The times are simulated.
32 devices in a mesh: gx: 8 (over y, x, core), gy: 4 (over z).
Axes of the slice: x: 2, y: 2, z: 4, core: 2. Of those that a mesh axis runs over, the one named last changes fastest.
Arguments:
- e_field: float32 [3, 3, 2048, 2048], P(None, None, 'gx', 'gy'), may hold values from -6 to 6
- h_field: float32 [3, 3, 2048, 2048], P(None, None, 'gx', 'gy'), may hold values from -6 to 6
- material: int32 [3, 2048, 2048], P(None, 'gx', 'gy'), may hold values from 0 to 7
- eps_table: float32 [8], replicated, may hold values from 1 to 12
- src_pos: int32 [1024, 3], replicated, may hold values from 0 to 2047, as said below
- src_amp: float32 [1024], replicated, may hold values from -40 to 40
- freqs: float32 [2], replicated, may hold values from 0.3 to 2.8
Outputs:
- e_out: float32 [3, 3, 2048, 2048], P(None, None, 'gx', 'gy')
- h_out: float32 [3, 3, 2048, 2048], P(None, None, 'gx', 'gy')
- far_field: float32 [1024, 8, 2, 1024], P('gx', None, None, 'gy')
Inputs may be any that keep to these rules, and one draw needn't show every extreme that they name: `src_pos`: each row is a cell (layer, row, column) of the slab; several sources may share a cell.
All inputs are finite; a program needn't handle non-finite values.
Results may differ from a plain program's by a relative error of at most 0.0054.
Values may be sent and summed in bfloat16 or wider, within the bound.
A program may use at most 192 MiB of HBM per device.

v0:
```python
import math
import jax
import jax.numpy as jnp
from jax import lax
from jax.sharding import PartitionSpec as P

LZ = 3
FACE = 1
STEPS = 2
NF = 2
NA = 1024
NMAT = 8
courant = 0.5
source_rate = 0.7
zoom_factor = 4


def shifted(block, axis, distance):
    devices = range(lax.axis_size(axis))
    route = [(i - distance, i) for i in devices if i - distance in devices]
    return lax.ppermute(block, axis, route)


def chirp(freq_index, cell_index, period):
    remainder = jnp.remainder(freq_index * cell_index, period)
    phase_angle = remainder.astype(jnp.float32) * (2.0 * math.pi / period)
    return (jnp.cos(phase_angle), -jnp.sin(phase_angle))


def forward(field, dimension, boundary):
    inner = lax.slice_in_dim(field, 1, field.shape[dimension], axis=dimension)
    return jnp.concatenate([inner, jnp.expand_dims(boundary, dimension)], dimension)


def backward(field, dimension, boundary):
    inner = lax.slice_in_dim(field, 0, field.shape[dimension] - 1, axis=dimension)
    return jnp.concatenate([jnp.expand_dims(boundary, dimension), inner], dimension)


def curl_forward(electric, row_rim, col_rim):
    field_x, field_y, field_z = (electric[0], electric[1], electric[2])
    zero_layer = jnp.zeros(field_x.shape[1:], jnp.float32)
    curl_x = forward(field_z, 2, col_rim[1]) - field_z - (forward(field_y, 0, zero_layer) - field_y)
    curl_y = forward(field_x, 0, zero_layer) - field_x - (forward(field_z, 1, row_rim[1]) - field_z)
    curl_z = forward(field_y, 1, row_rim[0]) - field_y - (forward(field_x, 2, col_rim[0]) - field_x)
    return jnp.stack([curl_x, curl_y, curl_z])


def curl_backward(magnetic, row_rim, col_rim):
    field_x, field_y, field_z = (magnetic[0], magnetic[1], magnetic[2])
    zero_layer = jnp.zeros(field_x.shape[1:], jnp.float32)
    curl_x = (
        field_z - backward(field_z, 2, col_rim[1]) - (field_y - backward(field_y, 0, zero_layer))
    )
    curl_y = (
        field_x - backward(field_x, 0, zero_layer) - (field_z - backward(field_z, 1, row_rim[1]))
    )
    curl_z = (
        field_y - backward(field_y, 1, row_rim[0]) - (field_x - backward(field_x, 2, col_rim[0]))
    )
    return jnp.stack([curl_x, curl_y, curl_z])


def complex_pair(product_re_re, product_re_im, product_im_re, product_im_im):
    return (product_re_re - product_im_im, product_re_im + product_im_re)


def on_device(e_field, h_field, material, eps_table, src_pos, src_amp, freqs):
    row_count = e_field.shape[2]
    col_count = e_field.shape[3]
    grid_rows = row_count * lax.axis_size("gx")
    grid_cols = col_count * lax.axis_size("gy")
    row_start = lax.axis_index("gx") * row_count
    col_start = lax.axis_index("gy") * col_count
    permittivity = jnp.zeros(material.shape, jnp.float32)
    for material_id in range(NMAT):
        permittivity = permittivity + jnp.where(
            material == material_id, eps_table[material_id], 0.0
        )
    update_scale = courant / permittivity
    local_row = src_pos[:, 1] - row_start
    local_col = src_pos[:, 2] - col_start
    inside = (local_row >= 0) & (local_row < row_count) & (local_col >= 0) & (local_col < col_count)
    kept_amp = jnp.where(inside, src_amp, 0.0)
    safe_row = jnp.clip(local_row, 0, row_count - 1)
    safe_col = jnp.clip(local_col, 0, col_count - 1)
    source_grid = (
        jnp.zeros((LZ, row_count, col_count), jnp.float32)
        .at[src_pos[:, 0], safe_row, safe_col]
        .add(kept_amp)
    )
    electric, magnetic = (e_field, h_field)
    real_sum = jnp.zeros((NF, 4, row_count, col_count), jnp.float32)
    imag_sum = jnp.zeros((NF, 4, row_count, col_count), jnp.float32)
    for step_index in range(STEPS):
        moment = float(step_index + 1)
        row_e = shifted(electric[1:3, :, 0, :], "gx", -1)
        col_e = shifted(electric[0::2, :, :, 0], "gy", -1)
        magnetic = magnetic - courant * curl_forward(electric, row_e, col_e)
        row_h = shifted(magnetic[1:3, :, row_count - 1, :], "gx", 1)
        col_h = shifted(magnetic[0::2, :, :, col_count - 1], "gy", 1)
        electric = electric + update_scale * curl_backward(magnetic, row_h, col_h)
        electric = electric.at[2].add(math.sin(source_rate * moment) * source_grid)
        face_now = jnp.stack(
            [-magnetic[1, FACE], magnetic[0, FACE], electric[1, FACE], -electric[0, FACE]]
        )
        real_sum = real_sum + face_now[None] * jnp.cos(freqs * moment)[:, None, None, None]
        imag_sum = imag_sum + face_now[None] * jnp.sin(freqs * moment)[:, None, None, None]
    item_count = NF * 4
    currents = jnp.stack(
        [
            real_sum.reshape(item_count, row_count, col_count),
            imag_sum.reshape(item_count, row_count, col_count),
        ],
        1,
    ).astype(jnp.bfloat16)
    angle_index = jnp.arange(NA, dtype=jnp.int32)
    y_cells = col_start + jnp.arange(col_count, dtype=jnp.int32)
    y_real, y_imag = chirp(
        y_cells[:, None], (angle_index + NA // 4)[None, :], zoom_factor * grid_cols
    )
    y_table = jnp.concatenate([y_real, y_imag], 1).astype(jnp.bfloat16)
    flipped = jnp.swapaxes(currents, 2, 3)
    all_rows = jnp.arange(grid_rows, dtype=jnp.int32)
    x_real, x_imag = chirp(
        (angle_index - NA // 2)[None, :], all_rows[:, None], zoom_factor * grid_rows
    )
    x_table = jnp.concatenate([x_real, x_imag], 1).astype(jnp.bfloat16)
    product = jnp.einsum(
        "kbcx,xw->kbcw",
        lax.all_to_all(flipped, "gx", split_axis=2, concat_axis=3, tiled=True),
        x_table,
        preferred_element_type=jnp.float32,
    )
    part_re, part_im = complex_pair(
        product[:, 0, :, :NA], product[:, 0, :, NA:], product[:, 1, :, :NA], product[:, 1, :, NA:]
    )
    transformed = jnp.stack([part_re, part_im], 1).astype(jnp.bfloat16)
    sectioned = lax.all_to_all(transformed, "gx", split_axis=3, concat_axis=2, tiled=True)
    second = jnp.einsum("ibcu,cw->uibw", sectioned, y_table, preferred_element_type=jnp.float32)
    far_re, far_im = complex_pair(
        second[:, :, 0, :NA], second[:, :, 0, NA:], second[:, :, 1, :NA], second[:, :, 1, NA:]
    )
    partial_far = jnp.stack([far_re, far_im], 2)
    inv_norm = 1.0 / math.sqrt(grid_rows * grid_cols)
    far_field = lax.psum_scatter(partial_far, "gy", scatter_dimension=3, tiled=True) * inv_norm
    return (electric, magnetic, far_field)


def solution(mesh):
    placed = (
        P(None, None, "gx", "gy"),
        P(None, None, "gx", "gy"),
        P(None, "gx", "gy"),
        P(),
        P(),
        P(),
        P(),
    )
    return jax.shard_map(
        on_device,
        mesh=mesh,
        in_specs=placed,
        out_specs=(P(None, None, "gx", "gy"), P(None, None, "gx", "gy"), P("gx", None, None, "gy")),
        check_vma=False,
    )
```

profile of v0, /device:TPU:0, one launch (start us, length us, event | category | flops | bytes accessed | tf_op | source)
XLA Modules:
  0.0 508.1 jit_solution(7167283156874817417)
XLA Ops:
  12.3 3.0 slice_bitcast_fusion.26
  15.3 3.5 slice_bitcast_fusion.17
  19.7 7.1 %scatter_custom_fusion = f32[393216]{0:T(1024)} fusion(s32[1024]{0:T(1024)S(1)} %broadcast_select_fusion, f32[1024]{0:T(1024)S(1)} %broadcast_select_fusion.1, f32[]{:T(128)} %constant.104.clone.1), kind=kCustom, calls=%fused_computation.121 | custom fusion | flops 1024 | bytes 1572868
  26.8 2.9 broadcast_multiply_fusion.1
  29.8 1.6 slice_bitcast_fusion.8
  33.3 6.3 %add_divide_fusion = f32[3,256,512]{2,1,0:T(8,128)S(1)} fusion(s32[3,256,512]{2,1,0:T(8,128)S(1)} %copy-done.32, f32[]{:T(128)} %bitcast.7, f32[]{:T(128)} %bitcast.6, f32[]{:T(128)} %bitcast.5, f32[]{:T(128)} %bitcast.4, f32[]{:T(128)} %bitcast.3, f32[]{:T(128)} %bitcast.2, f32[]{:T(128)} %bitcast.1, f32[]{:T(128)} %bitcast), kind=kLoop, calls=%fused_computation.101 | loop fusion | flops 9437184 | bytes 3145760 | tf_op jit(solution)/shard_map/div | solution.py:80
  42.6 2.6 reshape.245
  47.0 4.4 slice_bitcast_fusion.10
  62.7 3.0 collective-permute-start.3
  67.2 6.1 %collective-permute-start.2 = (f32[2,3,256]{2,0,1:T(2,128)S(1)}, f32[2,3,256]{2,0,1:T(2,128)S(1)}, u32[]{:S(2)}, u32[]{:S(2)}) collective-permute-start(f32[2,3,256]{2,0,1:T(2,128)S(1)} %bitcast.243), channel_id=1, source_target_pairs={{0,1},{1,2},{2,3},{4,5},{5,6},{6,7},{8,9},{9,10},{10,11},{12,13},{... | collective-permute-start | bytes 18440 | tf_op jit(solution)/shard_map/ppermute | solution.py:21
  73.3 2.7 slice_bitcast_fusion.6
  77.7 4.3 slice_bitcast_fusion.7
  90.4 1.6 slice.464
  93.3 2.0 slice_bitcast_fusion.13
  100.1 3.1 slice_bitcast_fusion.3
  106.7 2.9 copy.110
  109.5 4.1 mul.206
  113.7 7.7 %mul.207 = f32[8,1,256,512]{2,1,0,3:T(1,128)} reshape(f32[2,4,256,512]{2,1,0,3:T(4,128)} %mul.206) | data formatting | bytes 8388608 | tf_op jit(solution)/shard_map/mul | solution.py:107
  122.6 3.8 fusion.35
  127.7 2.8 fusion.32
  130.9 1.8 fusion.11
  137.3 3.8 collective-permute-start.7
  142.5 4.5 collective-permute-start.6
  150.2 3.8 slice_bitcast_fusion.2
  158.8 2.2 copy-done.11
  163.6 2.1 copy.111
  165.7 2.6 mul.212
  168.3 7.7 %mul.213 = f32[8,1,256,512]{2,1,0,3:T(1,128)} reshape(f32[2,4,256,512]{2,1,0,3:T(4,128)} %mul.212) | data formatting | bytes 8388608 | tf_op jit(solution)/shard_map/mul | solution.py:107
  176.1 10.6 %add_convert_fusion.1 = (bf16[8,1,256,512]{2,1,0,3:T(2,128)(2,1)S(1)}, bf16[8,1,256,512]{2,1,0,3:T(2,128)(2,1)S(1)}) fusion(f32[8,1,256,512]{2,1,0,3:T(1,128)} %mul.213, f32[8,1,256,512]{2,1,0,3:T(1,128)} %mul.207, f32[8]{0:T(128)S(1)} %copy-done.40, f32[8]{0:T(128)S(1)} %copy-done.37, f32[8]{0:T(128)S(1)} %copy-done.38, f32[8]{0:T(128)S(1)} %copy-done.39), kind=kLoop, calls=%fused_computation.30 | loop fusion | flops 8388608 | bytes 12583040 | tf_op jit(solution)/shard_map/convert.4
  186.7 10.5 %maximum_bitcast_fusion.2 = bf16[8,2,512,256]{3,1,0,2:T(2,128)(2,1)} fusion(bf16[8,1,256,512]{2,1,0,3:T(2,128)(2,1)S(1)} %get-tuple-element.47, bf16[8,1,256,512]{2,1,0,3:T(2,128)(2,1)S(1)} %get-tuple-element.46), kind=kLoop, calls=%fused_computation.28 | loop fusion | flops 8388608 | bytes 8388608 | tf_op jit(solution)/shard_map/transpose | solution.py:123
  197.2 6.2 %all-to-all-start = ((bf16[8,2,512,256]{3,1,0,2:T(2,128)(2,1)}), bf16[8,2,512,256]{3,1,0,2:T(2,128)(2,1)}, u32[]{:S(2)}, u32[]{:S(2)}) async-start(bf16[8,2,512,256]{3,1,0,2:T(2,128)(2,1)} %maximum_bitcast_fusion.2), calls=%async_computation | async-start | bytes 8388608 | tf_op jit(solution)/shard_map/all_to_all | solution.py:131
  203.4 35.0 %cosine_convert_fusion = (bf16[2048,1024]{1,0:T(8,128)(2,1)}, bf16[2048,1024]{1,0:T(8,128)(2,1)}) fusion(s32[1024]{0:T(1024)S(1)} %iota_add_fusion), kind=kLoop, calls=%fused_computation.13 | loop fusion | flops 35651584 | bytes 8392704 | tf_op jit(solution)/shard_map/convert.2
  238.4 14.1 %all-to-all-done = bf16[8,2,512,256]{3,1,0,2:T(2,128)(2,1)} async-done(((bf16[8,2,512,256]{3,1,0,2:T(2,128)(2,1)}), bf16[8,2,512,256]{3,1,0,2:T(2,128)(2,1)}, u32[]{:S(2)}, u32[]{:S(2)}) %all-to-all-start) | async-done | bytes 4194336 | tf_op jit(solution)/shard_map/all_to_all | solution.py:131
  252.5 3.7 copy.112
  259.7 8.8 %fusion.3 = f32[8,2,64,2048]{3,2,1,0:T(8,128)S(1)} fusion(bf16[8,2,64,2048]{3,2,1,0:T(8,128)(2,1)S(1)} %bitcast.236, bf16[2048,1024]{1,0:T(8,128)(2,1)S(1)} %copy-done.20, bf16[2048,1024]{1,0:T(8,128)(2,1)S(1)} %copy-done.19), kind=kOutput, calls=%fused_computation.8 | convolution fusion | flops 8606711808 | bytes 20971520 | tf_op jit(solution)/shard_map/kbcx,xw->kbcw/dot_general | solution.py:129
  269.5 7.8 %copy.114 = bf16[8,2,64,1024]{2,1,0,3:T(2,128)(2,1)} copy(bf16[8,2,64,1024]{3,2,1,0:T(8,128)(2,1)S(1)} %pad_maximum_fusion.3) | data formatting | bytes 4194304 | tf_op jit(solution)/shard_map/stack | solution.py:138
  277.3 7.6 %reshape.268 = bf16[8,2,65536]{2,1,0:T(2,128)(2,1)} reshape(bf16[1024,8,2,64]{3,2,1,0:T(2,128)(2,1)} %bitcast.229) | data formatting | bytes 4194304
  284.8 3.6 all-to-all-start.1
  288.8 9.8 %cosine_convert_fusion.1 = (bf16[512,1024]{0,1:T(8,128)(2,1)S(1)}, bf16[512,1024]{0,1:T(8,128)(2,1)}) fusion(s32[1024]{0:T(1024)S(1)} %iota_add_fusion.1, s32[512]{0:T(512)S(1)} %iota_add_fusion.2), kind=kLoop, calls=%fused_computation.50 | loop fusion | flops 8912896 | bytes 2103296 | tf_op jit(solution)/shard_map/convert.6
  298.6 16.4 %all-to-all-done.1 = bf16[8,2,65536]{2,1,0:T(2,128)(2,1)S(1)} async-done(((bf16[8,2,65536]{2,1,0:T(2,128)(2,1)}), bf16[8,2,65536]{2,1,0:T(2,128)(2,1)S(1)}, u32[]{:S(2)}, u32[]{:S(2)}) %all-to-all-start.1) | async-done | bytes 2097184 | tf_op jit(solution)/shard_map/all_to_all | solution.py:139
  315.0 5.0 reshape.269
  320.0 9.2 %copy.115 = bf16[8,2,64,8,128]{4,2,3,1,0:T(8,128)(2,1)S(1)} copy(bf16[8,2,64,8,128]{2,1,0,4,3:T(2,128)(2,1)} %bitcast.230) | data formatting | bytes 4194304 | tf_op jit(solution)/shard_map/all_to_all | solution.py:139
  329.2 9.4 %convolution_bitcast_fusion = f32[128,8,2,2048]{0,3,2,1:T(8,128)} fusion(bf16[8,2,512,128]{3,2,1,0:T(8,128)(2,1)S(1)} %bitcast.237, bf16[512,1024]{0,1:T(8,128)(2,1)} %get-tuple-element.102, bf16[512,1024]{0,1:T(8,128)(2,1)S(1)} %get-tuple-element.101), kind=kOutput, calls=%fused_computation.17 | convolution fusion | flops 4299161600 | bytes 20971520 | tf_op jit(solution)/shard_map/ibcu,cw->uibw/dot_general | solution.py:140
  338.6 8.7 %slice_subtract_fusion = (f32[128,8,1,1024]{0,3,2,1:T(8,128)S(1)}, f32[128,8,1,1024]{0,3,2,1:T(8,128)}) fusion(f32[128,8,2,2048]{0,3,2,1:T(8,128)} %convolution_bitcast_fusion), kind=kLoop, calls=%fused_computation.27 | loop fusion | flops 2097152 | bytes 25165824 | tf_op jit(solution)/shard_map/sub | solution.py:65
  347.3 6.2 %pad_maximum_fusion = f32[128,8,2,1024]{0,3,2,1:T(8,128)} fusion(f32[128,8,1,1024]{0,3,2,1:T(8,128)} %get-tuple-element.43, f32[128,8,1,1024]{0,3,2,1:T(8,128)S(1)} %get-tuple-element.42), kind=kLoop, calls=%fused_computation.11 | loop fusion | flops 2097152 | bytes 16777216 | tf_op jit(solution)/shard_map/stack | solution.py:144
  353.5 143.1 %reduce-scatter.2.cloned.1.call-done = f32[128,8,2,256]{0,3,2,1:T(8,128)} async-done(((f32[128,8,2,1024]{0,3,2,1:T(8,128)}), f32[128,8,2,256]{0,3,2,1:T(8,128)}) %reduce-scatter.2.cloned.1.call-update) | async-done | bytes 2097168 | tf_op jit(solution)/shard_map/reduce_scatter | solution.py:146
  496.7 1.8 broadcast_multiply_fusion
  498.5 2.3 copy.116
  (223 shorter events, 68.6 us)
Async XLA Ops:
  7.2 5.0 copy-start.35
  8.1 38.9 %collective-permute-start.1 = (f32[2,3,512]{2,0,1:T(2,128)S(1)}, f32[2,3,512]{2,0,1:T(2,128)S(1)}, u32[]{:S(2)}, u32[]{:S(2)}) collective-permute-start(f32[2,3,512]{2,0,1:T(2,128)S(1)} %bitcast.238), channel_id=1, source_target_pairs={{4,0},{8,4},{12,8},{16,12},{20,16},{24,20},{28,24},{5,1},{9,5},{13... | collective-permute-start | bytes 36872 | tf_op jit(solution)/shard_map/ppermute | solution.py:21
  10.9 35.7 %collective-permute-start = (f32[2,3,256]{2,0,1:T(2,128)S(1)}, f32[2,3,256]{2,0,1:T(2,128)S(1)}, u32[]{:S(2)}, u32[]{:S(2)}) collective-permute-start(f32[2,3,256]{2,0,1:T(2,128)S(1)} %bitcast.241), channel_id=1, source_target_pairs={{1,0},{2,1},{3,2},{5,4},{6,5},{7,6},{9,8},{10,9},{11,10},{13,12},{... | collective-permute-start | bytes 18440 | tf_op jit(solution)/shard_map/ppermute | solution.py:21
  15.3 3.5 copy-start.34
  15.3 4.2 copy-start.41
  15.3 4.3 copy-start.43
  15.3 4.4 copy-start.36
  26.8 2.9 copy-start.14
  33.3 6.3 %copy-start.42 = (f32[2]{0:T(128)S(1)}, f32[2]{0:T(128)}, u32[]{:S(2)}) copy-start(f32[2]{0:T(128)} %param.17) | copy-start | bytes 28
  39.6 44.6 %copy-start.9 = (f32[3,256,512]{2,1,0:T(8,128)}, f32[3,256,512]{2,1,0:T(8,128)S(1)}, u32[]{:S(2)}) copy-start(f32[3,256,512]{2,1,0:T(8,128)S(1)} %add_divide_fusion) | copy-start | bytes 4718596
  47.0 5.2 %slice-start.8 = ((s8[4718592]{0:T(1024)(128)(4,1)}), s8[4194304]{0:T(1024)(128)(4,1)S(1)}, s32[]{:S(2)}) async-start(s8[4718592]{0:T(1024)(128)(4,1)} %bitcast.221), calls=%async_computation.12 | async-start | bytes 8388608
  47.0 5.2 %slice-start.9 = ((s8[4718592]{0:T(1024)(128)(4,1)}), s8[524288]{0:T(1024)(128)(4,1)S(1)}, s32[]{:S(2)}) async-start(s8[4718592]{0:T(1024)(128)(4,1)} %bitcast.221), calls=%async_computation.13 | async-start | bytes 1048576
  51.5 3.5 copy-start.3
  56.9 4.4 copy-start.1
  62.7 14.9 %collective-permute-start.3 = (f32[2,3,512]{2,0,1:T(2,128)S(1)}, f32[2,3,512]{2,0,1:T(2,128)S(1)}, u32[]{:S(2)}, u32[]{:S(2)}) collective-permute-start(f32[2,3,512]{2,0,1:T(2,128)S(1)} %bitcast.239), channel_id=1, source_target_pairs={{0,4},{4,8},{8,12},{12,16},{16,20},{20,24},{24,28},{1,5},{5,9},{9,... | collective-permute-start | bytes 36872 | tf_op jit(solution)/shard_map/ppermute | solution.py:21
  67.2 10.1 %collective-permute-start.2 = (f32[2,3,256]{2,0,1:T(2,128)S(1)}, f32[2,3,256]{2,0,1:T(2,128)S(1)}, u32[]{:S(2)}, u32[]{:S(2)}) collective-permute-start(f32[2,3,256]{2,0,1:T(2,128)S(1)} %bitcast.243), channel_id=1, source_target_pairs={{0,1},{1,2},{2,3},{4,5},{5,6},{6,7},{8,9},{9,10},{10,11},{12,13},{... | collective-permute-start | bytes 18440 | tf_op jit(solution)/shard_map/ppermute | solution.py:21
  77.6 4.5 slice-start.4
  77.7 4.6 slice-start.5
  77.7 4.9 copy-start.23
  77.7 5.2 %copy-start.24 = (f32[2,256,512]{2,1,0:T(8,128)S(1)}, f32[2,256,512]{2,1,0:T(8,128)}, u32[]{:S(2)}) copy-start(f32[2,256,512]{2,1,0:T(8,128)} %get-tuple-element.75) | copy-start | bytes 3145732
  86.4 6.8 %copy-start = (f32[3,3,256,512]{3,2,1,0:T(8,128)}, f32[3,3,256,512]{3,2,1,0:T(8,128)S(1)}, u32[]{:S(2)}) copy-start(f32[3,3,256,512]{3,2,1,0:T(8,128)S(1)} %get-tuple-element.51) | copy-start | bytes 14155780
  95.9 26.7 %collective-permute-start.5 = (f32[2,3,512]{2,0,1:T(2,128)}, f32[2,3,512]{2,0,1:T(2,128)S(1)}, u32[]{:S(2)}, u32[]{:S(2)}) collective-permute-start(f32[2,3,512]{2,0,1:T(2,128)} %bitcast.205), channel_id=1, source_target_pairs={{4,0},{8,4},{12,8},{16,12},{20,16},{24,20},{28,24},{5,1},{9,5},{13... | collective-permute-start | bytes 36872 | tf_op jit(solution)/shard_map/ppermute | solution.py:21
  98.6 22.8 %collective-permute-start.4 = (f32[2,3,256]{2,0,1:T(2,128)S(1)}, f32[2,3,256]{2,0,1:T(2,128)S(1)}, u32[]{:S(2)}, u32[]{:S(2)}) collective-permute-start(f32[2,3,256]{2,0,1:T(2,128)S(1)} %bitcast.242), channel_id=1, source_target_pairs={{1,0},{2,1},{3,2},{5,4},{6,5},{7,6},{9,8},{10,9},{11,10},{13,12},{... | collective-permute-start | bytes 18440 | tf_op jit(solution)/shard_map/ppermute | solution.py:21
  100.1 3.2 copy-start.15
  122.4 4.1 slice-start
  122.6 4.1 slice-start.1
  122.6 4.6 copy-start.16
  122.6 5.0 copy-start.17
  122.6 5.0 copy-start.33
  126.5 4.1 slice-start.14
  127.7 2.9 copy-start.4
  127.7 2.9 copy-start.6
  127.7 3.2 copy-start.8
  132.7 4.3 copy-start.2
  137.3 12.6 %collective-permute-start.7 = (f32[2,3,512]{2,0,1:T(2,128)S(1)}, f32[2,3,512]{2,0,1:T(2,128)S(1)}, u32[]{:S(2)}, u32[]{:S(2)}) collective-permute-start(f32[2,3,512]{2,0,1:T(2,128)S(1)} %bitcast.240), channel_id=1, source_target_pairs={{0,4},{4,8},{8,12},{12,16},{16,20},{20,24},{24,28},{1,5},{5,9},{9,... | collective-permute-start | bytes 36872 | tf_op jit(solution)/shard_map/ppermute | solution.py:21
  142.5 7.0 %collective-permute-start.6 = (f32[2,3,256]{2,0,1:T(2,128)S(1)}, f32[2,3,256]{2,0,1:T(2,128)S(1)}, u32[]{:S(2)}, u32[]{:S(2)}) collective-permute-start(f32[2,3,256]{2,0,1:T(2,128)S(1)} %bitcast.244), channel_id=1, source_target_pairs={{0,1},{1,2},{2,3},{4,5},{5,6},{6,7},{8,9},{9,10},{10,11},{12,13},{... | collective-permute-start | bytes 18440 | tf_op jit(solution)/shard_map/ppermute | solution.py:21
  149.9 4.1 slice-start.6
  150.2 3.9 slice-start.7
  150.2 4.2 copy-start.25
  150.2 4.5 copy-start.26
  168.3 7.7 %copy-start.37 = (f32[8]{0:T(128)S(1)}, f32[8]{0:T(128)}, u32[]{:S(2)}) copy-start(f32[8]{0:T(128)} %mul.209) | copy-start | bytes 100
  168.3 7.7 %copy-start.38 = (f32[8]{0:T(128)S(1)}, f32[8]{0:T(128)}, u32[]{:S(2)}) copy-start(f32[8]{0:T(128)} %mul.224) | copy-start | bytes 100
  168.3 7.7 %copy-start.39 = (f32[8]{0:T(128)S(1)}, f32[8]{0:T(128)}, u32[]{:S(2)}) copy-start(f32[8]{0:T(128)} %mul.220) | copy-start | bytes 100
  168.3 7.7 %copy-start.40 = (f32[8]{0:T(128)S(1)}, f32[8]{0:T(128)}, u32[]{:S(2)}) copy-start(f32[8]{0:T(128)} %mul.216) | copy-start | bytes 100
  197.2 55.3 %all-to-all-start = ((bf16[8,2,512,256]{3,1,0,2:T(2,128)(2,1)}), bf16[8,2,512,256]{3,1,0,2:T(2,128)(2,1)}, u32[]{:S(2)}, u32[]{:S(2)}) async-start(bf16[8,2,512,256]{3,1,0,2:T(2,128)(2,1)} %maximum_bitcast_fusion.2), calls=%async_computation | async-start | bytes 8388608 | tf_op jit(solution)/shard_map/all_to_all | solution.py:131
  256.2 3.5 copy-start.20
  284.8 30.2 %all-to-all-start.1 = ((bf16[8,2,65536]{2,1,0:T(2,128)(2,1)}), bf16[8,2,65536]{2,1,0:T(2,128)(2,1)S(1)}, u32[]{:S(2)}, u32[]{:S(2)}) async-start(bf16[8,2,65536]{2,1,0:T(2,128)(2,1)} %reshape.268), calls=%async_computation.1 | async-start | bytes 4194304 | tf_op jit(solution)/shard_map/all_to_all | solution.py:139
  288.4 208.3 %reduce-scatter.2.cloned.1.call-start = ((), (), s32[]{:S(2)}) async-start(), calls=%async_computation.3 | async-start | bytes 10485760 | tf_op jit(solution)/shard_map/reduce_scatter | solution.py:146
  (23 other events, 42.1 us)
Sparse Core Ops, SparseCore 0:
  353.7 142.9 reduce-scatter.1
where the time goes:
time: 518 us; the launch traced here: 508 us
  waiting for transfers between devices  174 us (34%)
  other arithmetic  137 us (26%)
  local copies, waits for them, and re-layouts  130 us (25%)
  starting transfers between devices  32.9 us (6%)
  matrix products  18.3 us (4%)
  between operations  15.4 us (3%)
    reduce_scatter x1, waiting for transfers between devices, on_device(): lax.psum_scatter(partial_far, 'gy', scatter_dimension=3, tiled=True)  143 us
    another operation x4, other arithmetic  56.2 us
    unnamed x125, local copies, waits for them, and re-layouts  29.4 us
    mul x8, local copies, waits for them, and re-layouts, on_device(): face_now[None] * jnp.cos(freqs * moment)[:, None, None, None]  23.7 us
    ppermute x8, starting transfers between devices, shifted(): return lax.ppermute(block, axis, route)  22.7 us
    all_to_all x1, waiting for transfers between devices, on_device(): lax.all_to_all(transformed, 'gx', split_axis=3, concat_axis=2, tiled=True)  16.4 us
    all_to_all x1, waiting for transfers between devices, on_device(): lax.all_to_all(flipped, 'gx', split_axis=2, concat_axis=3, tiled=True)  14.1 us
    transpose x1, other arithmetic, on_device(): flipped = jnp.swapaxes(currents, 2, 3)  10.5 us
  transfers between devices with their start and end apart: 11, of which 3 were waited for; matrix products, arithmetic and copies ran while one was open for 22% of the time, Pallas kernels for 0%

commit v1 on v0

--- a/solution.py
+++ b/solution.py
@@ -136,7 +136,10 @@
         product[:, 0, :, :NA], product[:, 0, :, NA:], product[:, 1, :, :NA], product[:, 1, :, NA:]
     )
     transformed = jnp.stack([part_re, part_im], 1).astype(jnp.bfloat16)
-    sectioned = lax.all_to_all(transformed, "gx", split_axis=3, concat_axis=2, tiled=True)
+    sectioned = jnp.concatenate(
+        lax.all_to_all(jnp.stack(jnp.split(transformed, lax.axis_size("gx"), axis=3)), "gx", 0, 0),
+        axis=2,
+    )
     second = jnp.einsum("ibcu,cw->uibw", sectioned, y_table, preferred_element_type=jnp.float32)
     far_re, far_im = complex_pair(
         second[:, :, 0, :NA], second[:, :, 0, NA:], second[:, :, 1, :NA], second[:, :, 1, NA:]

time: 518 us -> 495 us (0.956)
  local copies, waits for them, and re-layouts: 130 us -> 102 us
  other arithmetic: 137 us -> 143 us
    unnamed x125, local copies, waits for them, and re-layouts: 29.4 us -> 17.9 us
    all_to_all x1 -> x0, local copies, waits for them, and re-layouts: 9.16 us -> none  [on_device(): lax.all_to_all(transformed, 'gx', split_axis=3, concat_axis=2, tiled=True)]
    another operation x3 -> x2, local copies, waits for them, and re-layouts: 11.8 us -> 4.02 us  [the longest x1 7.77 us: on_device(): transformed = jnp.stack([part_re, part_im], 1).astype(jnp.bfloat16)]
    unnamed x12 -> x19, other arithmetic: 7.3 us -> 12.7 us
  transfers between devices with their start and end apart: 11 -> 11, of which waited for: 3 -> 3; matrix products, arithmetic and copies ran while one was open for 22% -> 23% of each run, Pallas kernels for 0% -> 0%
where the time goes in v1:
time: 495 us; the launch traced here: 486 us
  waiting for transfers between devices  174 us (35%)
  other arithmetic  143 us (29%)
  local copies, waits for them, and re-layouts  102 us (21%)
  starting transfers between devices  33 us (7%)
  matrix products  18.3 us (4%)
  between operations  15.4 us (3%)
    reduce_scatter x1, waiting for transfers between devices, on_device(): lax.psum_scatter(partial_far, 'gy', scatter_dimension=3, tiled=True)  143 us
    another operation x4, other arithmetic  56.2 us
    mul x8, local copies, waits for them, and re-layouts, on_device(): face_now[None] * jnp.cos(freqs * moment)[:, None, None, None]  23.8 us
    ppermute x8, starting transfers between devices, shifted(): return lax.ppermute(block, axis, route)  22.9 us
    unnamed x125, local copies, waits for them, and re-layouts  17.9 us
    all_to_all x1, waiting for transfers between devices, on_device(): lax.all_to_all(jnp.stack(jnp.split(transformed, lax.axis_size('gx'), axis...  16.4 us
    all_to_all x1, waiting for transfers between devices, on_device(): lax.all_to_all(flipped, 'gx', split_axis=2, concat_axis=3, tiled=True)  14.1 us
    unnamed x19, other arithmetic  12.7 us
  transfers between devices with their start and end apart: 11, of which 3 were waited for; matrix products, arithmetic and copies ran while one was open for 23% of the time, Pallas kernels for 0%

profile of v1, /device:TPU:0, one launch (start us, length us, event | category | flops | bytes accessed | tf_op | source)
XLA Modules:
  0.0 485.7 jit_solution(10039564590289005132)
XLA Ops:
  12.3 3.0 slice_bitcast_fusion.26
  15.3 3.5 slice_bitcast_fusion.17
  19.7 7.1 %scatter_custom_fusion = f32[393216]{0:T(1024)} fusion(s32[1024]{0:T(1024)S(1)} %broadcast_select_fusion, f32[1024]{0:T(1024)S(1)} %broadcast_select_fusion.1, f32[]{:T(128)} %constant.104.clone.1), kind=kCustom, calls=%fused_computation.134 | custom fusion | flops 1024 | bytes 1572868
  26.8 2.9 broadcast_multiply_fusion.1
  29.7 1.6 slice_bitcast_fusion.8
  33.3 6.2 %add_divide_fusion = f32[3,256,512]{2,1,0:T(8,128)S(1)} fusion(s32[3,256,512]{2,1,0:T(8,128)S(1)} %copy-done.32, f32[]{:T(128)} %bitcast.7, f32[]{:T(128)} %bitcast.6, f32[]{:T(128)} %bitcast.5, f32[]{:T(128)} %bitcast.4, f32[]{:T(128)} %bitcast.3, f32[]{:T(128)} %bitcast.2, f32[]{:T(128)} %bitcast.1, f32[]{:T(128)} %bitcast), kind=kLoop, calls=%fused_computation.114 | loop fusion | flops 9437184 | bytes 3145760 | tf_op jit(solution)/shard_map/div | solution.py:80
  42.5 2.6 reshape.251
  47.0 4.4 slice_bitcast_fusion.10
  59.6 1.6 slice_bitcast_fusion.24
  62.7 3.0 collective-permute-start.3
  67.1 6.1 %collective-permute-start.2 = (f32[2,3,256]{2,0,1:T(2,128)S(1)}, f32[2,3,256]{2,0,1:T(2,128)S(1)}, u32[]{:S(2)}, u32[]{:S(2)}) collective-permute-start(f32[2,3,256]{2,0,1:T(2,128)S(1)} %bitcast.256), channel_id=1, source_target_pairs={{0,1},{1,2},{2,3},{4,5},{5,6},{6,7},{8,9},{9,10},{10,11},{12,13},{... | collective-permute-start | bytes 18440 | tf_op jit(solution)/shard_map/ppermute | solution.py:21
  73.2 2.7 slice_bitcast_fusion.6
  77.6 4.3 slice_bitcast_fusion.7
  90.4 1.6 slice.464
  93.2 2.0 slice_bitcast_fusion.13
  98.5 1.6 collective-permute-start.4
  100.1 3.0 slice_bitcast_fusion.3
  105.1 1.5 pad_maximum_fusion.1
  106.6 2.9 copy.109
  109.5 4.1 mul.206
  113.6 7.7 %mul.207 = f32[8,1,256,512]{2,1,0,3:T(1,128)} reshape(f32[2,4,256,512]{2,1,0,3:T(4,128)} %mul.206) | data formatting | bytes 8388608 | tf_op jit(solution)/shard_map/mul | solution.py:107
  122.6 3.8 fusion.35
  127.6 2.8 fusion.32
  130.8 1.8 fusion.11
  137.2 3.8 collective-permute-start.7
  142.4 4.5 collective-permute-start.6
  150.1 3.8 slice_bitcast_fusion.2
  158.7 2.2 copy-done.11
  163.5 2.1 copy.110
  165.6 2.6 mul.212
  168.2 7.7 %mul.213 = f32[8,1,256,512]{2,1,0,3:T(1,128)} reshape(f32[2,4,256,512]{2,1,0,3:T(4,128)} %mul.212) | data formatting | bytes 8388608 | tf_op jit(solution)/shard_map/mul | solution.py:107
  176.0 10.6 %add_convert_fusion.1 = (bf16[8,1,256,512]{2,1,0,3:T(2,128)(2,1)S(1)}, bf16[8,1,256,512]{2,1,0,3:T(2,128)(2,1)S(1)}) fusion(f32[8,1,256,512]{2,1,0,3:T(1,128)} %mul.213, f32[8,1,256,512]{2,1,0,3:T(1,128)} %mul.207, f32[8]{0:T(128)S(1)} %copy-done.41, f32[8]{0:T(128)S(1)} %copy-done.38, f32[8]{0:T(128)S(1)} %copy-done.39, f32[8]{0:T(128)S(1)} %copy-done.40), kind=kLoop, calls=%fused_computation.30 | loop fusion | flops 8388608 | bytes 12583040 | tf_op jit(solution)/shard_map/convert.4
  186.6 10.5 %maximum_bitcast_fusion.2 = bf16[8,2,512,256]{3,1,0,2:T(2,128)(2,1)} fusion(bf16[8,1,256,512]{2,1,0,3:T(2,128)(2,1)S(1)} %get-tuple-element.47, bf16[8,1,256,512]{2,1,0,3:T(2,128)(2,1)S(1)} %get-tuple-element.46), kind=kLoop, calls=%fused_computation.28 | loop fusion | flops 8388608 | bytes 8388608 | tf_op jit(solution)/shard_map/transpose | solution.py:123
  197.1 6.2 %all-to-all-start = ((bf16[8,2,512,256]{3,1,0,2:T(2,128)(2,1)}), bf16[8,2,512,256]{3,1,0,2:T(2,128)(2,1)}, u32[]{:S(2)}, u32[]{:S(2)}) async-start(bf16[8,2,512,256]{3,1,0,2:T(2,128)(2,1)} %maximum_bitcast_fusion.2), calls=%async_computation | async-start | bytes 8388608 | tf_op jit(solution)/shard_map/all_to_all | solution.py:131
  203.3 35.0 %cosine_convert_fusion = (bf16[2048,1024]{1,0:T(8,128)(2,1)}, bf16[2048,1024]{1,0:T(8,128)(2,1)}) fusion(s32[1024]{0:T(1024)S(1)} %iota_add_fusion), kind=kLoop, calls=%fused_computation.13 | loop fusion | flops 35651584 | bytes 8392704 | tf_op jit(solution)/shard_map/convert.2
  238.3 14.1 %all-to-all-done = bf16[8,2,512,256]{3,1,0,2:T(2,128)(2,1)} async-done(((bf16[8,2,512,256]{3,1,0,2:T(2,128)(2,1)}), bf16[8,2,512,256]{3,1,0,2:T(2,128)(2,1)}, u32[]{:S(2)}, u32[]{:S(2)}) %all-to-all-start) | async-done | bytes 4194336 | tf_op jit(solution)/shard_map/all_to_all | solution.py:131
  252.4 3.7 copy.111
  256.7 1.6 copy-done.19
  259.6 8.8 %fusion.3 = f32[8,2,64,2048]{3,2,1,0:T(8,128)S(1)} fusion(bf16[8,2,64,2048]{3,2,1,0:T(8,128)(2,1)S(1)} %bitcast.249, bf16[2048,1024]{1,0:T(8,128)(2,1)S(1)} %copy-done.20, bf16[2048,1024]{1,0:T(8,128)(2,1)S(1)} %copy-done.19), kind=kOutput, calls=%fused_computation.8 | convolution fusion | flops 8606711808 | bytes 20971520 | tf_op jit(solution)/shard_map/kbcx,xw->kbcw/dot_general | solution.py:129
  275.4 3.6 all-to-all-start.1
  279.4 9.8 %cosine_convert_fusion.1 = (bf16[512,1024]{0,1:T(8,128)(2,1)S(1)}, bf16[512,1024]{0,1:T(8,128)(2,1)}) fusion(s32[1024]{0:T(1024)S(1)} %iota_add_fusion.1, s32[512]{0:T(512)S(1)} %iota_add_fusion.2), kind=kLoop, calls=%fused_computation.63 | loop fusion | flops 8912896 | bytes 2103296 | tf_op jit(solution)/shard_map/convert.6
  289.2 16.4 %all-to-all-done.1 = bf16[8,8,2,64,128]{4,3,2,1,0:T(8,128)(2,1)S(1)} async-done(((bf16[8,8,2,64,128]{4,3,2,1,0:T(8,128)(2,1)}), bf16[8,8,2,64,128]{4,3,2,1,0:T(8,128)(2,1)S(1)}, u32[]{:S(2)}, u32[]{:S(2)}) %all-to-all-start.1) | async-done | bytes 2097184 | tf_op jit(solution)/shard_map/all_to_all | solution.py:140
  306.8 9.5 %convolution_bitcast_fusion = f32[128,8,2,2048]{0,3,2,1:T(8,128)} fusion(bf16[8,2,512,128]{3,2,1,0:T(8,128)(2,1)S(1)} %bitcast.250, bf16[512,1024]{0,1:T(8,128)(2,1)S(1)} %copy-done.34, bf16[512,1024]{0,1:T(8,128)(2,1)S(1)} %get-tuple-element.101), kind=kOutput, calls=%fused_computation.17 | convolution fusion | flops 4299161600 | bytes 20971520 | tf_op jit(solution)/shard_map/ibcu,cw->uibw/dot_general | solution.py:143
  316.2 8.7 %slice_subtract_fusion = (f32[128,8,1,1024]{0,3,2,1:T(8,128)S(1)}, f32[128,8,1,1024]{0,3,2,1:T(8,128)}) fusion(f32[128,8,2,2048]{0,3,2,1:T(8,128)} %convolution_bitcast_fusion), kind=kLoop, calls=%fused_computation.27 | loop fusion | flops 2097152 | bytes 25165824 | tf_op jit(solution)/shard_map/sub | solution.py:65
  324.9 6.2 %pad_maximum_fusion = f32[128,8,2,1024]{0,3,2,1:T(8,128)} fusion(f32[128,8,1,1024]{0,3,2,1:T(8,128)} %get-tuple-element.43, f32[128,8,1,1024]{0,3,2,1:T(8,128)S(1)} %get-tuple-element.42), kind=kLoop, calls=%fused_computation.11 | loop fusion | flops 2097152 | bytes 16777216 | tf_op jit(solution)/shard_map/stack | solution.py:147
  331.1 143.1 %reduce-scatter.2.cloned.1.call-done = f32[128,8,2,256]{0,3,2,1:T(8,128)} async-done(((f32[128,8,2,1024]{0,3,2,1:T(8,128)}), f32[128,8,2,256]{0,3,2,1:T(8,128)}) %reduce-scatter.2.cloned.1.call-update) | async-done | bytes 2097168 | tf_op jit(solution)/shard_map/reduce_scatter | solution.py:149
  474.3 1.8 broadcast_multiply_fusion
  476.1 2.3 copy.114
  (229 shorter events, 69.7 us)
Async XLA Ops:
  7.2 5.0 %copy-start.36 = (s32[1024,3]{0,1:T(4,128)S(1)}, s32[1024,3]{0,1:T(4,128)}, u32[]{:S(2)}) copy-start(s32[1024,3]{0,1:T(4,128)} %param.15) | copy-start | bytes 36868
  8.1 38.8 %collective-permute-start.1 = (f32[2,3,512]{2,0,1:T(2,128)S(1)}, f32[2,3,512]{2,0,1:T(2,128)S(1)}, u32[]{:S(2)}, u32[]{:S(2)}) collective-permute-start(f32[2,3,512]{2,0,1:T(2,128)S(1)} %bitcast.251), channel_id=1, source_target_pairs={{4,0},{8,4},{12,8},{16,12},{20,16},{24,20},{28,24},{5,1},{9,5},{13... | collective-permute-start | bytes 36872 | tf_op jit(solution)/shard_map/ppermute | solution.py:21
  10.9 35.7 %collective-permute-start = (f32[2,3,256]{2,0,1:T(2,128)S(1)}, f32[2,3,256]{2,0,1:T(2,128)S(1)}, u32[]{:S(2)}, u32[]{:S(2)}) collective-permute-start(f32[2,3,256]{2,0,1:T(2,128)S(1)} %bitcast.254), channel_id=1, source_target_pairs={{1,0},{2,1},{3,2},{5,4},{6,5},{7,6},{9,8},{10,9},{11,10},{13,12},{... | collective-permute-start | bytes 18440 | tf_op jit(solution)/shard_map/ppermute | solution.py:21
  15.3 3.5 copy-start.35
  15.3 4.2 copy-start.42
  15.3 4.3 copy-start.44
  15.3 4.4 copy-start.37
  26.8 2.9 copy-start.14
  32.7 6.8 %copy-start.43 = (f32[2]{0:T(128)S(1)}, f32[2]{0:T(128)}, u32[]{:S(2)}) copy-start(f32[2]{0:T(128)} %param.17) | copy-start | bytes 28
  39.5 44.7 %copy-start.9 = (f32[3,256,512]{2,1,0:T(8,128)}, f32[3,256,512]{2,1,0:T(8,128)S(1)}, u32[]{:S(2)}) copy-start(f32[3,256,512]{2,1,0:T(8,128)S(1)} %add_divide_fusion) | copy-start | bytes 4718596
  47.0 5.2 %slice-start.8 = ((s8[4718592]{0:T(1024)(128)(4,1)}), s8[4194304]{0:T(1024)(128)(4,1)S(1)}, s32[]{:S(2)}) async-start(s8[4718592]{0:T(1024)(128)(4,1)} %bitcast.235), calls=%async_computation.12 | async-start | bytes 8388608
  47.0 5.2 %slice-start.9 = ((s8[4718592]{0:T(1024)(128)(4,1)}), s8[524288]{0:T(1024)(128)(4,1)S(1)}, s32[]{:S(2)}) async-start(s8[4718592]{0:T(1024)(128)(4,1)} %bitcast.235), calls=%async_computation.13 | async-start | bytes 1048576
  51.4 3.5 copy-start.3
  56.9 4.4 copy-start.1
  62.7 14.9 %collective-permute-start.3 = (f32[2,3,512]{2,0,1:T(2,128)S(1)}, f32[2,3,512]{2,0,1:T(2,128)S(1)}, u32[]{:S(2)}, u32[]{:S(2)}) collective-permute-start(f32[2,3,512]{2,0,1:T(2,128)S(1)} %bitcast.252), channel_id=1, source_target_pairs={{0,4},{4,8},{8,12},{12,16},{16,20},{20,24},{24,28},{1,5},{5,9},{9,... | collective-permute-start | bytes 36872 | tf_op jit(solution)/shard_map/ppermute | solution.py:21
  67.1 10.0 %collective-permute-start.2 = (f32[2,3,256]{2,0,1:T(2,128)S(1)}, f32[2,3,256]{2,0,1:T(2,128)S(1)}, u32[]{:S(2)}, u32[]{:S(2)}) collective-permute-start(f32[2,3,256]{2,0,1:T(2,128)S(1)} %bitcast.256), channel_id=1, source_target_pairs={{0,1},{1,2},{2,3},{4,5},{5,6},{6,7},{8,9},{9,10},{10,11},{12,13},{... | collective-permute-start | bytes 18440 | tf_op jit(solution)/shard_map/ppermute | solution.py:21
  77.6 4.5 slice-start.4
  77.6 4.6 slice-start.5
  77.6 4.9 %copy-start.23 = (f32[2,256,512]{2,1,0:T(8,128)S(1)}, f32[2,256,512]{2,1,0:T(8,128)}, u32[]{:S(2)}) copy-start(f32[2,256,512]{2,1,0:T(8,128)} %get-tuple-element.74) | copy-start | bytes 3145732
  77.6 5.2 %copy-start.24 = (f32[2,256,512]{2,1,0:T(8,128)S(1)}, f32[2,256,512]{2,1,0:T(8,128)}, u32[]{:S(2)}) copy-start(f32[2,256,512]{2,1,0:T(8,128)} %get-tuple-element.75) | copy-start | bytes 3145732
  86.4 6.8 %copy-start = (f32[3,3,256,512]{3,2,1,0:T(8,128)}, f32[3,3,256,512]{3,2,1,0:T(8,128)S(1)}, u32[]{:S(2)}) copy-start(f32[3,3,256,512]{3,2,1,0:T(8,128)S(1)} %get-tuple-element.51) | copy-start | bytes 14155780
  95.8 26.7 %collective-permute-start.5 = (f32[2,3,512]{2,0,1:T(2,128)}, f32[2,3,512]{2,0,1:T(2,128)S(1)}, u32[]{:S(2)}, u32[]{:S(2)}) collective-permute-start(f32[2,3,512]{2,0,1:T(2,128)} %bitcast.219), channel_id=1, source_target_pairs={{4,0},{8,4},{12,8},{16,12},{20,16},{24,20},{28,24},{5,1},{9,5},{13... | collective-permute-start | bytes 36872 | tf_op jit(solution)/shard_map/ppermute | solution.py:21
  98.5 4.6 copy-start.15
  98.5 22.8 %collective-permute-start.4 = (f32[2,3,256]{2,0,1:T(2,128)S(1)}, f32[2,3,256]{2,0,1:T(2,128)S(1)}, u32[]{:S(2)}, u32[]{:S(2)}) collective-permute-start(f32[2,3,256]{2,0,1:T(2,128)S(1)} %bitcast.255), channel_id=1, source_target_pairs={{1,0},{2,1},{3,2},{5,4},{6,5},{7,6},{9,8},{10,9},{11,10},{13,12},{... | collective-permute-start | bytes 18440 | tf_op jit(solution)/shard_map/ppermute | solution.py:21
  122.3 4.1 slice-start
  122.5 4.1 slice-start.1
  122.5 4.6 copy-start.16
  122.5 5.0 %copy-start.17 = (f32[3,256,511]{2,1,0:T(8,128)S(1)}, f32[3,256,511]{2,1,0:T(8,128)}, u32[]{:S(2)}) copy-start(f32[3,256,511]{2,1,0:T(8,128)} %slice.464) | copy-start | bytes 4709380
  122.5 5.0 %copy-start.33 = (f32[3,256,1]{2,1,0:T(8,128)S(1)}, f32[3,256,1]{2,1,0:T(8,128)}, u32[]{:S(2)}) copy-start(f32[3,256,1]{2,1,0:T(8,128)} %copy.101) | copy-start | bytes 9220
  126.4 4.1 slice-start.14
  127.6 2.9 copy-start.4
  127.6 2.9 copy-start.6
  127.6 3.2 copy-start.8
  132.6 4.3 copy-start.2
  137.2 12.6 %collective-permute-start.7 = (f32[2,3,512]{2,0,1:T(2,128)S(1)}, f32[2,3,512]{2,0,1:T(2,128)S(1)}, u32[]{:S(2)}, u32[]{:S(2)}) collective-permute-start(f32[2,3,512]{2,0,1:T(2,128)S(1)} %bitcast.253), channel_id=1, source_target_pairs={{0,4},{4,8},{8,12},{12,16},{16,20},{20,24},{24,28},{1,5},{5,9},{9,... | collective-permute-start | bytes 36872 | tf_op jit(solution)/shard_map/ppermute | solution.py:21
  142.4 7.0 %collective-permute-start.6 = (f32[2,3,256]{2,0,1:T(2,128)S(1)}, f32[2,3,256]{2,0,1:T(2,128)S(1)}, u32[]{:S(2)}, u32[]{:S(2)}) collective-permute-start(f32[2,3,256]{2,0,1:T(2,128)S(1)} %bitcast.257), channel_id=1, source_target_pairs={{0,1},{1,2},{2,3},{4,5},{5,6},{6,7},{8,9},{9,10},{10,11},{12,13},{... | collective-permute-start | bytes 18440 | tf_op jit(solution)/shard_map/ppermute | solution.py:21
  149.8 4.1 slice-start.6
  150.1 3.9 slice-start.7
  150.1 4.2 copy-start.25
  150.1 4.5 copy-start.26
  168.2 7.7 %copy-start.38 = (f32[8]{0:T(128)S(1)}, f32[8]{0:T(128)}, u32[]{:S(2)}) copy-start(f32[8]{0:T(128)} %mul.209) | copy-start | bytes 100
  168.2 7.7 %copy-start.39 = (f32[8]{0:T(128)S(1)}, f32[8]{0:T(128)}, u32[]{:S(2)}) copy-start(f32[8]{0:T(128)} %mul.224) | copy-start | bytes 100
  168.2 7.7 %copy-start.40 = (f32[8]{0:T(128)S(1)}, f32[8]{0:T(128)}, u32[]{:S(2)}) copy-start(f32[8]{0:T(128)} %mul.220) | copy-start | bytes 100
  168.2 7.7 %copy-start.41 = (f32[8]{0:T(128)S(1)}, f32[8]{0:T(128)}, u32[]{:S(2)}) copy-start(f32[8]{0:T(128)} %mul.216) | copy-start | bytes 100
  197.1 55.3 %all-to-all-start = ((bf16[8,2,512,256]{3,1,0,2:T(2,128)(2,1)}), bf16[8,2,512,256]{3,1,0,2:T(2,128)(2,1)}, u32[]{:S(2)}, u32[]{:S(2)}) async-start(bf16[8,2,512,256]{3,1,0,2:T(2,128)(2,1)} %maximum_bitcast_fusion.2), calls=%async_computation | async-start | bytes 8388608 | tf_op jit(solution)/shard_map/all_to_all | solution.py:131
  256.1 3.5 copy-start.20
  275.4 30.2 %all-to-all-start.1 = ((bf16[8,8,2,64,128]{4,3,2,1,0:T(8,128)(2,1)}), bf16[8,8,2,64,128]{4,3,2,1,0:T(8,128)(2,1)S(1)}, u32[]{:S(2)}, u32[]{:S(2)}) async-start(bf16[8,8,2,64,128]{4,3,2,1,0:T(8,128)(2,1)} %fusion.57), calls=%async_computation.1 | async-start | bytes 4194304 | tf_op jit(solution)/shard_map/all_to_all | solution.py:140
  279.0 195.3 %reduce-scatter.2.cloned.1.call-start = ((), (), s32[]{:S(2)}) async-start(), calls=%async_computation.3 | async-start | bytes 10485760 | tf_op jit(solution)/shard_map/reduce_scatter | solution.py:149
  (24 other events, 43.3 us)
Sparse Core Ops, SparseCore 0:
  331.3 142.9 reduce-scatter.1
